TPU v7x, 32 devices: a whole 2x2x4 slice. The times are simulated.
32 devices in a mesh: groups: 2 (over y), feat: 4 (over z), dp: 2 (over x), section: 2 (over core).
Axes of the slice: x: 2, y: 2, z: 4, core: 2. Of those that a mesh axis runs over, the one named last changes fastest.
Arguments:
- residuals: bfloat16 [2, 3072, 8192], P('section', ('groups', 'dp'), 'feat'), parts along dimension 1, may hold values from -6 to 6
- final_resid: bfloat16 [3072, 8192], P(('groups', 'dp', 'section'), 'feat'), parts along dimension 0, may hold values from -6 to 6
- final_order: int32 [3072], P(('groups', 'dp')), parts along dimension 0, may hold values from 0 to 767, as said below
- translator: bfloat16 [2, 8192, 8192], P('section', 'dp', 'feat'), may hold values from -0.0625 to 0.0625
- bias: float32 [2, 8192], P('section', 'feat'), may hold values from -5 to 5
Outputs:
- grad_weight: bfloat16 [4, 8192, 8192], P(('groups', 'section'), 'dp', 'feat'), parts along dimension 0
- grad_bias: float32 [4, 8192], P(('groups', 'section'), 'feat'), parts along dimension 0
There are 2 independent parts, one for each index of `groups`. A program takes and returns all parts, laid end to end along the dimension named above; an argument that names none is the same for every part. Nothing has to cross between parts.
Inputs may be any that keep to these rules, and one draw needn't show every extreme that they name: Within each aligned block of 768 tokens final_order is a permutation of 0 to 767.
All inputs are finite; a program needn't handle non-finite values.
Results may differ from a plain program's by a relative error of at most 0.0058.
Values may be sent and summed in bfloat16 or wider, within the bound.
A program may use at most 192 MiB of HBM per device.

v0:
```python
import math

import jax
import jax.numpy as jnp
from jax import lax
from jax.sharding import PartitionSpec as P


def on_device(residuals, final_resid, final_order, translator, bias):
    layer_rows = residuals[0]
    local_weight = translator[0]
    gathered_final = lax.all_gather(final_resid, "section", axis=0, tiled=True)
    targets = gathered_final[final_order].astype(jnp.float32)
    full_weight = lax.all_gather(local_weight, "dp", axis=0, tiled=True)
    gathered = lax.all_gather(layer_rows, "feat", axis=1, tiled=True)
    product = jnp.dot(gathered, full_weight, preferred_element_type=jnp.float32)
    predicted = layer_rows.astype(jnp.float32) + product + bias[0]
    token_total = layer_rows.shape[0] * lax.axis_size("dp")
    factor = 1.0 / math.sqrt(token_total)
    scaled_error = (predicted - targets) * factor
    grad_b = lax.psum(jnp.sum(scaled_error, axis=0), "dp")
    rounded = scaled_error.astype(jnp.bfloat16)
    partial_sum = lax.dot_general(
        gathered, rounded, (((0,), (0,)), ((), ())), preferred_element_type=jnp.float32
    )
    partial_sum = lax.optimization_barrier(partial_sum.astype(jnp.bfloat16))
    grad_w = lax.psum_scatter(
        partial_sum.astype(jnp.float32).astype(jnp.bfloat16), "dp", scatter_dimension=0, tiled=True
    )
    return (grad_w[None], grad_b[None])


def solution(mesh):
    placed = (
        P("section", ("groups", "dp"), "feat"),
        P(("groups", "dp", "section"), "feat"),
        P(("groups", "dp")),
        P("section", "dp", "feat"),
        P("section", "feat"),
    )
    return jax.shard_map(
        on_device,
        mesh=mesh,
        in_specs=placed,
        out_specs=(P(("groups", "section"), "dp", "feat"), P(("groups", "section"), "feat")),
        check_vma=False,
    )
```

profile of v0, /device:TPU:0, one launch (start us, length us, event | category | flops | bytes accessed | tf_op | source)
XLA Modules:
  0.0 1101.7 jit_solution(1509310580802462595)
XLA Ops:
  7.2 0.0 all-gather.6.cloned.1.call-start
  7.2 0.7 all-gather.6.cloned.1.call-update
  7.9 0.0 all-gather.8.cloned.1.call-start
  7.9 0.7 all-gather.8.cloned.1.call-update
  8.6 0.0 copy-start.1
  8.7 0.0 all-gather.10.cloned.1.call-start
  8.7 0.7 all-gather.10.cloned.1.call-update
  9.4 0.0 reduce-scatter.2.cloned.1.call-start
  9.4 0.0 copy-done.1
  9.5 0.0 copy-start
  9.5 0.0 copy-start.2
  9.5 14.9 %all-gather.6.cloned.1.call-done = bf16[768,2048]{1,0:T(8,128)(2,1)} async-done(((bf16[384,2048]{1,0:T(8,128)(2,1)}), bf16[768,2048]{1,0:T(8,128)(2,1)}) %all-gather.6.cloned.1.call-update) | async-done | bytes 3145744 | tf_op jit(solution)/shard_map/all_gather | solution.py:12
  24.4 9.4 gather_fusion
  33.8 211.6 %all-gather.8.cloned.1.call-done = bf16[1,768,8192]{2,1,0:T(8,128)(2,1)} async-done(((bf16[1,768,2048]{2,1,0:T(8,128)(2,1)}), bf16[1,768,8192]{2,1,0:T(8,128)(2,1)}) %all-gather.8.cloned.1.call-update) | async-done | bytes 12582928 | tf_op jit(solution)/shard_map/all_gather | solution.py:15
  245.4 388.3 %all-gather.10.cloned.1.call-done = bf16[1,8192,2048]{2,1,0:T(8,128)(2,1)} async-done(((bf16[1,4096,2048]{2,1,0:T(8,128)(2,1)}), bf16[1,8192,2048]{2,1,0:T(8,128)(2,1)}) %all-gather.10.cloned.1.call-update) | async-done | bytes 33554448 | tf_op jit(solution)/shard_map/all_gather | solution.py:14
  633.7 0.0 copy-done
  633.7 0.0 copy-done.2
  633.7 34.7 %fusion.12 = (f32[2048]{0:T(1024)S(1)}, bf16[768,2048]{1,0:T(8,128)(2,1)S(1)}) fusion(bf16[768,2048]{1,0:T(8,128)(2,1)} %gather_fusion, f32[2048]{0:T(1024)S(1)} %bitcast.27, bf16[1,8192,2048]{2,1,0:T(8,128)(2,1)} %all-gather.10.cloned.1.call-done, bf16[1,768,8192]{2,1,0:T(8,128)(2,1)} %all-gather.8.cloned.1.call-done, bf16[1,768,2048]{2,1,0:T(8,128)(2,1)S(1)} %copy-done), kind=kOutput, calls=%fused_computation.13 | convolution fusion | flops 25782384640 | bytes 55590912 | tf_op jit(solution)/shard_map/dot_general | solution.py:16
  668.4 35.2 %convert_bitcast_fusion = bf16[8192,2048]{0,1:T(8,128)(2,1)} fusion(bf16[1,768,8192]{2,1,0:T(8,128)(2,1)} %all-gather.8.cloned.1.call-done, bf16[768,2048]{1,0:T(8,128)(2,1)S(1)} %get-tuple-element.5), kind=kOutput, calls=%fused_computation.3 | convolution fusion | flops 25786580992 | bytes 49283072 | tf_op jit(solution)/shard_map/dot_general | solution.py:23
  703.6 0.0 reduce-scatter.2.cloned.1.call-update
  703.7 5.6 psum.7
  709.3 363.5 %reduce-scatter.2.cloned.1.call-done = bf16[4096,2048]{0,1:T(8,128)(2,1)} async-done(((bf16[8192,2048]{0,1:T(8,128)(2,1)}), bf16[4096,2048]{0,1:T(8,128)(2,1)}) %reduce-scatter.2.cloned.1.call-update) | async-done | bytes 16777232 | tf_op jit(solution)/shard_map/reduce_scatter | solution.py:27
  1072.7 22.4 %copy.7 = bf16[1,4096,2048]{2,1,0:T(8,128)(2,1)} copy(bf16[1,4096,2048]{1,2,0:T(8,128)(2,1)} %bitcast.25) | data formatting | bytes 33554432
  (2 shorter events, 0.0 us)
Async XLA Ops:
  7.2 17.2 %all-gather.6.cloned.1.call-start = ((), (), s32[]{:S(2)}) async-start(), calls=%async_computation.1 | async-start | bytes 4718592 | tf_op jit(solution)/shard_map/all_gather | solution.py:12
  7.9 237.5 %all-gather.8.cloned.1.call-start = ((), (), s32[]{:S(2)}) async-start(), calls=%async_computation.3 | async-start | bytes 15728640 | tf_op jit(solution)/shard_map/all_gather | solution.py:15
  8.6 0.8 copy-start.1
  8.7 625.1 %all-gather.10.cloned.1.call-start = ((), (), s32[]{:S(2)}) async-start(), calls=%async_computation.4 | async-start | bytes 50331648 | tf_op jit(solution)/shard_map/all_gather | solution.py:14
  9.4 1063.3 %reduce-scatter.2.cloned.1.call-start = ((), (), s32[]{:S(2)}) async-start(), calls=%async_computation.2 | async-start | bytes 50331648 | tf_op jit(solution)/shard_map/reduce_scatter | solution.py:27
  9.5 624.2 %copy-start = (bf16[1,768,2048]{2,1,0:T(8,128)(2,1)S(1)}, bf16[1,768,2048]{2,1,0:T(8,128)(2,1)}, u32[]{:S(2)}) copy-start(bf16[1,768,2048]{2,1,0:T(8,128)(2,1)} %param.5) | copy-start | bytes 9437188
  9.5 624.2 %copy-start.2 = (f32[1,2048]{1,0:T(1,128)S(1)}, f32[1,2048]{1,0:T(1,128)}, u32[]{:S(2)}) copy-start(f32[1,2048]{1,0:T(1,128)} %param.9) | copy-start | bytes 24580
Sparse Core Ops, SparseCore 0:
  9.5 14.8 all-gather.5
  26.0 219.3 all-gather.7
  246.9 386.7 all-gather.9
  703.8 368.8 reduce-scatter.1
where the time goes:
time: 1100 us
  waiting for transfers between devices  980 us (89%)
  matrix products  69.9 us (6%)
  local copies, waits for them, and re-layouts  31.8 us (3%)
  between operations  13.8 us (1%)
    all_gather x1, waiting for transfers between devices, on_device(): full_weight = lax.all_gather(local_weight, 'dp', axis=0, tiled=True)  388 us
    reduce_scatter x1, waiting for transfers between devices, on_device(): lax.psum_scatter(partial_sum.astype(jnp.float32).astype(jnp.bfloat16), 'd...  363 us
    all_gather x1, waiting for transfers between devices, on_device(): gathered = lax.all_gather(layer_rows, 'feat', axis=1, tiled=True)  212 us
    dot_general x1, matrix products, on_device(): lax.dot_general(gathered, rounded, (((0,), (0,)), ((), ())), preferred_el...  35.2 us
    dot_general x1, matrix products, on_device(): product = jnp.dot(gathered, full_weight, preferred_element_type=jnp.float32)  34.7 us
    unnamed x7, local copies, waits for them, and re-layouts  22.4 us
  transfers between devices with their start and end apart: 4, of which 4 were waited for; matrix products, arithmetic and copies ran while one was open for 1% of the time, Pallas kernels for 0%

commit v1 on v0

v1 whole, which is shorter than its diff:
```python
import math

import jax
import jax.numpy as jnp
from jax import lax
from jax.sharding import PartitionSpec as P

CHUNKS = 2


def on_device(residuals, final_resid, final_order, translator, bias):
    own = residuals[0]
    weight = translator[0]
    tokens = own.shape[0]
    ways = lax.axis_size("dp")
    factor = 1.0 / math.sqrt(tokens * ways)
    gathered_final = lax.all_gather(final_resid, "section", axis=0, tiled=True)
    targets = gathered_final[final_order].astype(jnp.float32)
    step = tokens // CHUNKS
    inputs, errors = [], []
    grad_b = 0.0
    for c in range(CHUNKS):
        rows = slice(c * step, (c + 1) * step)
        wide = lax.all_gather(own[rows], "feat", axis=1, tiled=True)
        halves = jnp.stack(jnp.split(wide, ways, axis=1))
        mine = lax.all_to_all(halves, "dp", split_axis=0, concat_axis=0, tiled=True)
        mine = mine.reshape(ways * step, -1)
        part = jnp.dot(mine, weight, preferred_element_type=jnp.float32).astype(jnp.bfloat16)
        parts = lax.all_to_all(
            part.reshape(ways, step, -1), "dp", split_axis=0, concat_axis=0, tiled=True
        )
        product = jnp.sum(parts.astype(jnp.float32), axis=0)
        scaled = (own[rows].astype(jnp.float32) + product + bias[0] - targets[rows]) * factor
        grad_b = grad_b + jnp.sum(scaled, axis=0)
        inputs.append(mine)
        errors.append(lax.all_gather(scaled.astype(jnp.bfloat16), "dp", axis=0, tiled=True))
    grad_b = lax.psum(grad_b, "dp")
    grad_w = lax.dot_general(
        jnp.concatenate(inputs), jnp.concatenate(errors), (((0,), (0,)), ((), ())),
        preferred_element_type=jnp.float32,
    ).astype(jnp.bfloat16)
    return (grad_w[None], grad_b[None])


def solution(mesh):
    placed = (
        P("section", ("groups", "dp"), "feat"),
        P(("groups", "dp", "section"), "feat"),
        P(("groups", "dp")),
        P("section", "dp", "feat"),
        P("section", "feat"),
    )
    return jax.shard_map(
        on_device,
        mesh=mesh,
        in_specs=placed,
        out_specs=(P(("groups", "section"), "dp", "feat"), P(("groups", "section"), "feat")),
        check_vma=False,
    )
```

time: 1100 us -> 547 us (0.50)
  waiting for transfers between devices: 980 us -> 390 us
  starting transfers between devices: 0.15 us -> 22.8 us
  other arithmetic: 0.01 us -> 20.2 us
    reduce_scatter x1 -> x0, waiting for transfers between devices: 363 us -> none  [on_device(): lax.psum_scatter(partial_sum.astype(jnp.float32).astype(jnp.bfloat16), 'd...]
    all_gather x2 -> x4, waiting for transfers between devices: 600 us -> 301 us  [the longest x2 219 us: on_device(): wide = lax.all_gather(own[rows], 'feat', axis=1, tiled=True)]
    all_to_all x0 -> x4, waiting for transfers between devices: none -> 86.8 us  [the longest x2 50.7 us: on_device(): mine = lax.all_to_all(halves, 'dp', split_axis=0, concat_axis=0, tiled=True)]
    all_to_all x0 -> x4, starting transfers between devices: none -> 22.6 us  [the longest x2 13.3 us: on_device(): mine = lax.all_to_all(halves, 'dp', split_axis=0, concat_axis=0, tiled=True)]
    unnamed x7 -> x12, local copies, waits for them, and re-layouts: 22.4 us -> 2.21 us
    all_gather x1, waiting for transfers between devices: 14.9 us -> 0.02 us  [on_device(): gathered_final = lax.all_gather(final_resid, 'section', axis=0, tiled=True)]
    dot_general x2 -> x3, matrix products: 69.9 us -> 72.4 us  [the longest x2 39.4 us: on_device(): jnp.dot(mine, weight, preferred_element_type=jnp.float32)]
  transfers between devices with their start and end apart: 4 -> 9, of which waited for: 4 -> 7; matrix products, arithmetic and copies ran while one was open for 1% -> 12% of each run, Pallas kernels for 0% -> 0%
where the time goes in v1:
time: 547 us; the launch traced here: 546 us
  waiting for transfers between devices  390 us (71%)
  matrix products  72.4 us (13%)
  starting transfers between devices  22.8 us (4%)
  local copies, waits for them, and re-layouts  21.4 us (4%)
  other arithmetic  20.2 us (4%)
  between operations  13.9 us (3%)
  blocking collectives  5.82 us (1%)
    all_gather x2, waiting for transfers between devices, on_device(): wide = lax.all_gather(own[rows], 'feat', axis=1, tiled=True)  219 us
    all_gather x2, waiting for transfers between devices, on_device(): lax.all_gather(scaled.astype(jnp.bfloat16), 'dp', axis=0, tiled=True)  81.8 us
    all_to_all x2, waiting for transfers between devices, on_device(): mine = lax.all_to_all(halves, 'dp', split_axis=0, concat_axis=0, tiled=True)  50.7 us
    dot_general x2, matrix products, on_device(): jnp.dot(mine, weight, preferred_element_type=jnp.float32)  39.4 us
    all_to_all x2, waiting for transfers between devices, on_device(): lax.all_to_all(part.reshape(ways, step, -1), 'dp', split_axis=0, concat_a...  36.1 us
    dot_general x1, matrix products, on_device(): lax.dot_general(jnp.concatenate(inputs), jnp.concatenate(errors), (((0,),...  33 us
    all_to_all x2, starting transfers between devices, on_device(): mine = lax.all_to_all(halves, 'dp', split_axis=0, concat_axis=0, tiled=True)  13.3 us
  transfers between devices with their start and end apart: 9, of which 7 were waited for; matrix products, arithmetic and copies ran while one was open for 12% of the time, Pallas kernels for 0%

profile of v1, /device:TPU:0, one launch (start us, length us, event | category | flops | bytes accessed | tf_op | source)
XLA Modules:
  0.0 546.1 jit_solution(4865078908594601578)
XLA Ops:
  7.2 0.0 all-gather.14.cloned.1.call-start
  7.2 4.0 fusion.25
  11.2 0.0 all-gather.14.cloned.1.call-update
  11.2 0.0 all-gather.16.cloned.1.call-start
  11.3 0.7 all-gather.16.cloned.1.call-update
  12.0 117.5 %all-gather.14.cloned.1.call-done = bf16[1,384,8192]{2,1,0:T(8,128)(2,1)} async-done(((bf16[1,384,2048]{2,1,0:T(8,128)(2,1)}), bf16[1,384,8192]{2,1,0:T(8,128)(2,1)}) %all-gather.14.cloned.1.call-update) | async-done | bytes 6291472 | tf_op jit(solution)/shard_map/all_gather | solution.py:24
  129.4 3.3 slice_bitcast_fusion.3
  132.7 3.1 pad_maximum_fusion
  135.8 6.5 %all-to-all-start = ((bf16[2,384,4096]{2,1,0:T(8,128)(2,1)}), bf16[2,384,4096]{2,1,0:T(8,128)(2,1)}, u32[]{:S(2)}, u32[]{:S(2)}) async-start(bf16[2,384,4096]{2,1,0:T(8,128)(2,1)} %pad_maximum_fusion), calls=%async_computation | async-start | bytes 12582912 | tf_op jit(solution)/shard_map/all_to_all | solution.py:26
  142.3 0.0 all-gather.8.cloned.1.call-start
  142.4 0.7 all-gather.8.cloned.1.call-update
  143.0 101.5 %all-gather.16.cloned.1.call-done = bf16[1,384,8192]{2,1,0:T(8,128)(2,1)} async-done(((bf16[1,384,2048]{2,1,0:T(8,128)(2,1)}), bf16[1,384,8192]{2,1,0:T(8,128)(2,1)}) %all-gather.16.cloned.1.call-update) | async-done | bytes 6291472 | tf_op jit(solution)/shard_map/all_gather | solution.py:24
  244.6 3.3 slice_bitcast_fusion.1
  247.8 3.2 pad_maximum_fusion.1
  251.1 0.0 all-to-all-done
  251.1 6.8 %all-to-all-start.1 = ((bf16[2,384,4096]{2,1,0:T(8,128)(2,1)}), bf16[2,384,4096]{2,1,0:T(8,128)(2,1)}, u32[]{:S(2)}, u32[]{:S(2)}) async-start(bf16[2,384,4096]{2,1,0:T(8,128)(2,1)} %pad_maximum_fusion.1), calls=%async_computation.1 | async-start | bytes 12582912 | tf_op jit(solution)/shard_map/all_to_all | solution.py:26
  257.9 19.7 %fusion.10 = bf16[768,2048]{1,0:T(8,128)(2,1)} fusion(bf16[768,4096]{1,0:T(8,128)(2,1)} %bitcast.3, bf16[1,4096,2048]{2,1,0:T(8,128)(2,1)} %param.8), kind=kOutput, calls=%fused_computation.16 | convolution fusion | flops 12886474752 | bytes 26214400 | tf_op jit(solution)/shard_map/dot_general | solution.py:28
  277.6 50.7 %all-to-all-done.1 = bf16[2,384,4096]{2,1,0:T(8,128)(2,1)} async-done(((bf16[2,384,4096]{2,1,0:T(8,128)(2,1)}), bf16[2,384,4096]{2,1,0:T(8,128)(2,1)}, u32[]{:S(2)}, u32[]{:S(2)}) %all-to-all-start.1) | async-done | bytes 6291488 | tf_op jit(solution)/shard_map/all_to_all | solution.py:26
  328.3 4.1 all-to-all-start.2
  332.4 19.7 %fusion.13 = bf16[768,2048]{1,0:T(8,128)(2,1)} fusion(bf16[768,4096]{1,0:T(8,128)(2,1)} %bitcast.7, bf16[1,4096,2048]{2,1,0:T(8,128)(2,1)} %param.8), kind=kOutput, calls=%fused_computation.17 | convolution fusion | flops 12886474752 | bytes 26214400 | tf_op jit(solution)/shard_map/dot_general | solution.py:28
  352.2 15.9 %all-to-all-done.2 = bf16[2,384,2048]{2,1,0:T(8,128)(2,1)S(1)} async-done(((bf16[2,384,2048]{2,1,0:T(8,128)(2,1)}), bf16[2,384,2048]{2,1,0:T(8,128)(2,1)S(1)}, u32[]{:S(2)}, u32[]{:S(2)}) %all-to-all-start.2) | async-done | bytes 3145760 | tf_op jit(solution)/shard_map/all_to_all | solution.py:29
  368.0 0.0 copy-start.2
  368.0 0.0 copy-start.5
  368.0 1.7 copy-done.2
  369.7 5.2 all-to-all-start.3
  374.9 0.0 all-gather.12.cloned.1.call-start
  375.0 0.0 copy-done.5
  375.0 0.0 all-gather.8.cloned.1.call-done
  375.0 8.6 %gather_fusion = bf16[768,2048]{1,0:T(8,128)(2,1)S(1)} fusion(bf16[768,2048]{1,0:T(8,128)(2,1)} %all-gather.8.cloned.1.call-done, s32[1024]{0:T(1024)S(1)} %pad_clamp_fusion), kind=kCustom, calls=%fused_computation | custom fusion | bytes 6294528 | tf_op jit(solution)/shard_map/gather | solution.py:18
  383.7 0.0 copy-start.3
  383.7 3.5 convert_element_type.33
  387.2 0.0 copy-done.3
  387.2 0.0 copy-start.1
  387.2 0.0 copy-start.4
  387.2 2.4 convert_reduce_fusion.1
  389.6 20.2 %all-to-all-done.3 = bf16[2,384,2048]{2,1,0:T(8,128)(2,1)} async-done(((bf16[2,384,2048]{2,1,0:T(8,128)(2,1)}), bf16[2,384,2048]{2,1,0:T(8,128)(2,1)}, u32[]{:S(2)}, u32[]{:S(2)}) %all-to-all-start.3) | async-done | bytes 3145760 | tf_op jit(solution)/shard_map/all_to_all | solution.py:29
  409.9 0.0 copy-start
  409.9 3.2 convert_reduce_fusion
  413.0 0.0 copy-done.1
  413.1 0.0 copy-done.4
  413.1 0.5 copy-done
  413.6 4.7 fusion.23
  418.3 0.0 all-gather.12.cloned.1.call-update
  418.3 0.0 all-gather.10.cloned.1.call-start
  418.3 0.5 all-gather.10.cloned.1.call-update
  418.9 5.8 %psum.7 = f32[1,2048]{1,0:T(1,128)} all-reduce(f32[1,2048]{1,0:T(1,128)S(1)} %bitcast.47), channel_id=1, replica_groups=mesh['groups'=2,'feat'=4,'dp'=2,'section'=2] {'dp'}, use_global_device_ids=true, to_apply=%region_4.0 | all-reduce | flops 2048 | bytes 16384 | tf_op jit(solution)/shard_map/psum | solution.py:37
  424.7 35.5 %all-gather.12.cloned.1.call-done = bf16[768,2048]{1,0:T(8,128)(2,1)} async-done(((bf16[384,2048]{1,0:T(8,128)(2,1)}), bf16[768,2048]{1,0:T(8,128)(2,1)}) %all-gather.12.cloned.1.call-update) | async-done | bytes 3145744 | tf_op jit(solution)/shard_map/all_gather | solution.py:36
  460.2 46.4 %all-gather.10.cloned.1.call-done = bf16[768,2048]{1,0:T(8,128)(2,1)} async-done(((bf16[384,2048]{1,0:T(8,128)(2,1)}), bf16[768,2048]{1,0:T(8,128)(2,1)}) %all-gather.10.cloned.1.call-update) | async-done | bytes 3145744 | tf_op jit(solution)/shard_map/all_gather | solution.py:36
  506.5 33.0 %convert_bitcast_fusion = bf16[1,4096,2048]{2,1,0:T(8,128)(2,1)} fusion(bf16[768,4096]{1,0:T(8,128)(2,1)} %bitcast.7, bf16[768,4096]{1,0:T(8,128)(2,1)} %bitcast.3, bf16[768,2048]{1,0:T(8,128)(2,1)} %all-gather.12.cloned.1.call-done, bf16[768,2048]{1,0:T(8,128)(2,1)} %all-gather.10.cloned.1.call-done), kind=kOutput, calls=%fused_computation.5 | convolution fusion | flops 25815941120 | bytes 35651584 | tf_op jit(solution)/shard_map/dot_general | solution.py:38
  (3 shorter events, 0.0 us)
Async XLA Ops:
  7.2 122.3 %all-gather.14.cloned.1.call-start = ((), (), s32[]{:S(2)}) async-start(), calls=%async_computation.7 | async-start | bytes 7864320 | tf_op jit(solution)/shard_map/all_gather | solution.py:24
  11.2 233.3 %all-gather.16.cloned.1.call-start = ((), (), s32[]{:S(2)}) async-start(), calls=%async_computation.8 | async-start | bytes 7864320 | tf_op jit(solution)/shard_map/all_gather | solution.py:24
  135.8 115.3 %all-to-all-start = ((bf16[2,384,4096]{2,1,0:T(8,128)(2,1)}), bf16[2,384,4096]{2,1,0:T(8,128)(2,1)}, u32[]{:S(2)}, u32[]{:S(2)}) async-start(bf16[2,384,4096]{2,1,0:T(8,128)(2,1)} %pad_maximum_fusion), calls=%async_computation | async-start | bytes 12582912 | tf_op jit(solution)/shard_map/all_to_all | solution.py:26
  142.3 232.7 %all-gather.8.cloned.1.call-start = ((), (), s32[]{:S(2)}) async-start(), calls=%async_computation.4 | async-start | bytes 4718592 | tf_op jit(solution)/shard_map/all_gather | solution.py:17
  251.1 77.2 %all-to-all-start.1 = ((bf16[2,384,4096]{2,1,0:T(8,128)(2,1)}), bf16[2,384,4096]{2,1,0:T(8,128)(2,1)}, u32[]{:S(2)}, u32[]{:S(2)}) async-start(bf16[2,384,4096]{2,1,0:T(8,128)(2,1)} %pad_maximum_fusion.1), calls=%async_computation.1 | async-start | bytes 12582912 | tf_op jit(solution)/shard_map/all_to_all | solution.py:26
  328.3 39.7 %all-to-all-start.2 = ((bf16[2,384,2048]{2,1,0:T(8,128)(2,1)}), bf16[2,384,2048]{2,1,0:T(8,128)(2,1)S(1)}, u32[]{:S(2)}, u32[]{:S(2)}) async-start(bf16[2,384,2048]{2,1,0:T(8,128)(2,1)} %bitcast.46), calls=%async_computation.2 | async-start | bytes 6291456 | tf_op jit(solution)/shard_map/all_to_all | solution.py:29
  368.0 1.7 copy-start.2
  368.0 6.9 %copy-start.5 = (s32[768]{0:T(1024)S(1)}, s32[768]{0:T(1024)}, u32[]{:S(2)}) copy-start(s32[768]{0:T(1024)} %param.7) | copy-start | bytes 9220
  369.7 40.1 %all-to-all-start.3 = ((bf16[2,384,2048]{2,1,0:T(8,128)(2,1)}), bf16[2,384,2048]{2,1,0:T(8,128)(2,1)}, u32[]{:S(2)}, u32[]{:S(2)}) async-start(bf16[2,384,2048]{2,1,0:T(8,128)(2,1)} %bitcast.45), calls=%async_computation.3 | async-start | bytes 6291456 | tf_op jit(solution)/shard_map/all_to_all | solution.py:29
  374.9 85.3 %all-gather.12.cloned.1.call-start = ((), (), s32[]{:S(2)}) async-start(), calls=%async_computation.6 | async-start | bytes 4718592 | tf_op jit(solution)/shard_map/all_gather | solution.py:36
  383.7 3.6 copy-start.3
  387.2 25.8 %copy-start.1 = (bf16[1,768,2048]{2,1,0:T(8,128)(2,1)S(1)}, bf16[1,768,2048]{2,1,0:T(8,128)(2,1)}, u32[]{:S(2)}) copy-start(bf16[1,768,2048]{2,1,0:T(8,128)(2,1)} %param.5) | copy-start | bytes 9437188
  387.2 25.8 %copy-start.4 = (f32[1,2048]{1,0:T(1,128)S(1)}, f32[1,2048]{1,0:T(1,128)}, u32[]{:S(2)}) copy-start(f32[1,2048]{1,0:T(1,128)} %param.9) | copy-start | bytes 24580
  409.9 3.7 copy-start
  418.3 88.3 %all-gather.10.cloned.1.call-start = ((), (), s32[]{:S(2)}) async-start(), calls=%async_computation.5 | async-start | bytes 4718592 | tf_op jit(solution)/shard_map/all_gather | solution.py:36
Sparse Core Ops, SparseCore 0:
  11.3 118.0 all-gather.13
  131.0 113.5 all-gather.15
  246.1 10.3 all-gather.7
  418.4 41.7 all-gather.11
  461.6 44.9 all-gather.9

commit v2 on v1

--- a/solution.py
+++ b/solution.py
@@ -1,14 +1,356 @@
+import functools
 import math
 
 import jax
 import jax.numpy as jnp
 from jax import lax
+from jax.experimental import pallas as pl
+from jax.experimental.pallas import tpu as pltpu
 from jax.sharding import PartitionSpec as P
 
-CHUNKS = 2
-
-
-def on_device(residuals, final_resid, final_order, translator, bias):
+CHUNKS = 6
+MESH = pl.DeviceIdType.MESH
+
+
+def dot(a, b):
+    return jnp.dot(a, b, preferred_element_type=jnp.float32)
+
+
+def exchange_kernel(
+    chunks, factor, own_hbm, fin_hbm, order_ref, w_hbm, bias_ref,
+    x_out, e_out, gb_out,
+    slabs, transit, own, fin, w, p_send, p_recv, mine, err, gb,
+    load_sem, fin_sem, send_sem, recv_sem, p_sem, e_sem, gb_sem, out_sem,
+):
+    h = lax.axis_index("dp")
+    f = lax.axis_index("feat")
+    core = lax.axis_index("section")
+    way = 1 - 2 * h
+    g = f * way + 3 * h
+    outer, inner = h, 1 - h
+    tokens, width = own.shape
+    step = tokens // chunks
+    up, down, across = {"feat": f + way}, {"feat": f - way}, {"dp": 1 - h}
+    sibling = {"section": 1 - core}
+    half = fin_hbm.shape[0]
+
+    def rows(c):
+        return pl.ds(pl.multiple_of(c * step, step), step)
+
+    def place(k, c):
+        if k == 4:
+            return transit.at[rows(c)]
+        return slabs.at[(outer, outer, inner, inner)[k], k % 2, rows(c)]
+
+    def landing(k, c):
+        return slabs.at[(inner, inner, outer, outer)[k], k % 2, rows(c)]
+
+    def along(src, k, slot, to, c):
+        return pltpu.make_async_remote_copy(
+            src_ref=src, dst_ref=place(k, c), send_sem=send_sem.at[slot, c],
+            recv_sem=recv_sem.at[k, c], device_id=to, device_id_type=MESH)
+
+    def over(src, k, c):
+        return pltpu.make_async_remote_copy(
+            src_ref=src, dst_ref=landing(k, c), send_sem=send_sem.at[0, c],
+            recv_sem=recv_sem.at[k, c], device_id=across, device_id_type=MESH)
+
+    def rise(k, c, src=None):
+        return along(place(k, c) if src is None else src, k, 1 + k, up, c)
+
+    def sink(k, c, src=None):
+        return along(place(k, c) if src is None else src, k, 3 + k, down, c)
+
+    def arrived(k, c):
+        along(place(k, c), k, 0, across, c).wait_recv()
+
+    def at(*positions):
+        hit = g == positions[0]
+        for p in positions[1:]:
+            hit = jnp.logical_or(hit, g == p)
+        return pl.when(hit)
+
+    load_own = pltpu.make_async_copy(own_hbm, own, load_sem.at[0])
+    load_w = pltpu.make_async_copy(w_hbm, w, load_sem.at[1])
+    keep_outer = pltpu.make_async_copy(own_hbm, slabs.at[outer, 0], load_sem.at[2])
+    keep_inner = pltpu.make_async_copy(own_hbm, slabs.at[inner, 0], load_sem.at[2])
+    fin_rows = fin.at[pl.ds(pl.multiple_of(core * half, half), half)]
+    load_fin = pltpu.make_async_copy(fin_hbm, fin_rows, load_sem.at[3])
+    load_own.start()
+    load_fin.start()
+    at(0)(keep_outer.start)
+    at(1)(keep_inner.start)
+    load_w.start()
+    gb[0] = jnp.zeros_like(gb[0])
+
+    barrier = pltpu.get_barrier_semaphore()
+    for to in (across, sibling):
+        pl.semaphore_signal(barrier, inc=1, device_id=to, device_id_type=MESH)
+
+    @at(0, 1, 2)
+    def _():
+        pl.semaphore_signal(barrier, inc=1, device_id=up, device_id_type=MESH)
+
+    @at(1, 2, 3)
+    def _():
+        pl.semaphore_signal(barrier, inc=1, device_id=down, device_id_type=MESH)
+
+    @at(0, 3)
+    def _():
+        pl.semaphore_wait(barrier, 3)
+
+    @at(1, 2)
+    def _():
+        pl.semaphore_wait(barrier, 4)
+
+    load_own.wait()
+    load_fin.wait()
+    send_fin = pltpu.make_async_remote_copy(
+        src_ref=fin_rows, dst_ref=fin_rows, send_sem=fin_sem.at[0],
+        recv_sem=fin_sem.at[1], device_id=sibling, device_id_type=MESH)
+    send_fin.start()
+
+    def start_own(c):
+        src = own.at[rows(c)]
+
+        @at(0)
+        def _():
+            rise(0, c, src).start()
+
+        @at(1)
+        def _():
+            rise(2, c, src).start()
+            sink(2, c, src).start()
+
+        @at(2)
+        def _():
+            over(src, 3, c).start()
+
+        @at(3)
+        def _():
+            over(src, 1, c).start()
+            sink(4, c, src).start()
+
+    def forward(c):
+        @at(0)
+        def _():
+            arrived(1, c)
+            rise(1, c).start()
+            arrived(4, c)
+            over(place(4, c), 1, c).start()
+
+        @at(1)
+        def _():
+            arrived(0, c)
+            rise(0, c).start()
+            arrived(3, c)
+            rise(3, c).start()
+            sink(3, c).start()
+            arrived(4, c)
+            over(place(4, c), 1, c).start()
+            sink(4, c).start()
+
+        @at(2)
+        def _():
+            arrived(4, c)
+            sink(4, c).start()
+            for k in (0, 2, 3):
+                arrived(k, c)
+                rise(k, c).start()
+
+    def collect(c):
+        @at(0)
+        def _():
+            arrived(2, c)
+            arrived(3, c)
+
+        @at(1, 2)
+        def _():
+            arrived(1, c)
+
+        @at(3)
+        def _():
+            for k in range(4):
+                arrived(k, c)
+
+    def finish(c):
+        src = own.at[rows(c)]
+
+        @at(0)
+        def _():
+            rise(0, c, src).wait_send()
+            rise(1, c).wait_send()
+            over(place(4, c), 1, c).wait_send()
+
+        @at(1)
+        def _():
+            rise(2, c, src).wait_send()
+            sink(2, c, src).wait_send()
+            rise(0, c).wait_send()
+            rise(3, c).wait_send()
+            sink(3, c).wait_send()
+            over(place(4, c), 1, c).wait_send()
+            sink(4, c).wait_send()
+
+        @at(2)
+        def _():
+            over(src, 3, c).wait_send()
+            sink(4, c).wait_send()
+            for k in (0, 2, 3):
+                rise(k, c).wait_send()
+
+        @at(3)
+        def _():
+            over(src, 1, c).wait_send()
+            sink(4, c, src).wait_send()
+
+    def send_p(c):
+        return pltpu.make_async_remote_copy(
+            src_ref=p_send.at[rows(c)], dst_ref=p_recv.at[rows(c)], send_sem=p_sem.at[0, c],
+            recv_sem=p_sem.at[1, c], device_id=across, device_id_type=MESH)
+
+    def send_e(c):
+        return pltpu.make_async_remote_copy(
+            src_ref=err.at[0, rows(c)], dst_ref=err.at[1, rows(c)], send_sem=e_sem.at[0, c],
+            recv_sem=e_sem.at[1, c], device_id=across, device_id_type=MESH)
+
+    def keep_x(c):
+        return pltpu.make_async_copy(
+            slabs.at[:, :, rows(c)], x_out.at[:, :, rows(c)], out_sem.at[c])
+
+    tile = min(512, width)
+
+    def compute(c):
+        collect(c)
+        keep_x(c).start()
+
+        @pl.loop(0, width // tile)
+        def _(n):
+            cols = pl.ds(pl.multiple_of(n * tile, tile), tile)
+            other = dot(slabs[0, 1, rows(c)], w[0, :, cols]) + dot(slabs[1, 1, rows(c)], w[1, :, cols])
+            p_send[rows(c), cols] = other.astype(p_send.dtype)
+
+        send_p(c).start()
+        chosen = order_ref[rows(c)] == lax.broadcasted_iota(jnp.int32, (step, tokens), 1)
+        chosen = jnp.where(chosen, 1.0, 0.0).astype(fin.dtype)
+
+        @pl.loop(0, width // tile)
+        def _(n):
+            cols = pl.ds(pl.multiple_of(n * tile, tile), tile)
+            value = dot(slabs[0, 0, rows(c)], w[0, :, cols]) + dot(slabs[1, 0, rows(c)], w[1, :, cols])
+            target = dot(chosen, fin[:, cols])
+            mine[c % 2, :, cols] = own[rows(c), cols].astype(jnp.float32) + value + bias_ref[:, cols] - target
+
+    def settle(c):
+        send_p(c).wait_recv()
+
+        @pl.loop(0, width // tile)
+        def _(n):
+            cols = pl.ds(pl.multiple_of(n * tile, tile), tile)
+            scaled = (mine[c % 2, :, cols] + p_recv[rows(c), cols].astype(jnp.float32)) * factor
+            err[0, rows(c), cols] = scaled.astype(err.dtype)
+            gb[0, :, cols] += jnp.sum(scaled.reshape(step // 8, 8, tile), axis=0)
+
+        send_e(c).start()
+
+    start_own(0)
+    start_own(1)
+
+    @pl.loop(0, chunks + 2)
+    def _(s):
+        @pl.when(s + 2 < chunks)
+        def _():
+            start_own(s + 2)
+
+        @pl.when(s < chunks)
+        def _():
+            forward(s)
+
+        @pl.when(s == 1)
+        def _():
+            at(0)(keep_outer.wait)
+            at(1)(keep_inner.wait)
+            load_w.wait()
+            send_fin.wait()
+
+        @pl.when(jnp.logical_and(s >= 1, s <= chunks))
+        def _():
+            compute(s - 1)
+
+        @pl.when(s >= 2)
+        def _():
+            settle(s - 2)
+
+    send_gb = pltpu.make_async_remote_copy(
+        src_ref=gb.at[0], dst_ref=gb.at[1], send_sem=gb_sem.at[0], recv_sem=gb_sem.at[1],
+        device_id=across, device_id_type=MESH)
+    send_gb.start()
+
+    @pl.loop(0, chunks)
+    def _(c):
+        finish(c)
+        send_p(c).wait_send()
+        send_e(c).wait()
+        keep_x(c).wait()
+
+    send_gb.wait()
+    keep_e = pltpu.make_async_copy(err, e_out, load_sem.at[0])
+    keep_e.start()
+    gb_out[...] = jnp.sum(gb[0] + gb[1], axis=0, keepdims=True)
+    keep_e.wait()
+
+
+def paired(residuals, final_resid, final_order, translator, bias):
+    own = residuals[0]
+    tokens, width = own.shape
+    factor = 1.0 / math.sqrt(tokens * lax.axis_size("dp"))
+    weight = translator[0].reshape(2, width, -1)
+    bf16, f32 = own.dtype, jnp.float32
+    hbm = pl.BlockSpec(memory_space=pl.ANY)
+    vmem = pl.BlockSpec(memory_space=pltpu.VMEM)
+    dma = pltpu.SemaphoreType.DMA
+    x_all, e_all, grad_b = pl.pallas_call(
+        functools.partial(exchange_kernel, CHUNKS, factor),
+        out_shape=(
+            jax.ShapeDtypeStruct((2, 2, tokens, width), bf16),
+            jax.ShapeDtypeStruct((2, tokens, width), bf16),
+            jax.ShapeDtypeStruct((1, width), f32),
+        ),
+        in_specs=[hbm, hbm, vmem, hbm, vmem],
+        out_specs=(hbm, hbm, vmem),
+        scratch_shapes=[
+            pltpu.VMEM((2, 2, tokens, width), bf16),
+            pltpu.VMEM((tokens, width), bf16),
+            pltpu.VMEM((tokens, width), bf16),
+            pltpu.VMEM((tokens, width), bf16),
+            pltpu.VMEM(weight.shape, bf16),
+            pltpu.VMEM((tokens, width), bf16),
+            pltpu.VMEM((tokens, width), bf16),
+            pltpu.VMEM((2, tokens // CHUNKS, width), f32),
+            pltpu.VMEM((2, tokens, width), bf16),
+            pltpu.VMEM((2, 8, width), f32),
+            dma((4,)),
+            dma((2,)),
+            dma((8, CHUNKS)),
+            dma((5, CHUNKS)),
+            dma((2, CHUNKS)),
+            dma((2, CHUNKS)),
+            dma((2,)),
+            dma((CHUNKS,)),
+        ],
+        compiler_params=pltpu.CompilerParams(
+            collective_id=0, has_side_effects=True, vmem_limit_bytes=60 * 1024 * 1024),
+        name="exchange",
+    )(own, final_resid, final_order[:, None], weight, bias)
+    x_all = x_all.reshape(2, 2 * tokens, width)
+    e_all = e_all.reshape(2 * tokens, width)
+    grad_w = lax.dot_general(
+        x_all, e_all, (((1,), (0,)), ((), ())), preferred_element_type=f32
+    ).astype(bf16)
+    return grad_w.reshape(1, 2 * width, -1), grad_b
+
+
+def general(residuals, final_resid, final_order, translator, bias):
     own = residuals[0]
     weight = translator[0]
     tokens = own.shape[0]
@@ -16,16 +358,17 @@
     factor = 1.0 / math.sqrt(tokens * ways)
     gathered_final = lax.all_gather(final_resid, "section", axis=0, tiled=True)
     targets = gathered_final[final_order].astype(jnp.float32)
-    step = tokens // CHUNKS
+    chunks = 2
+    step = tokens // chunks
     inputs, errors = [], []
     grad_b = 0.0
-    for c in range(CHUNKS):
+    for c in range(chunks):
         rows = slice(c * step, (c + 1) * step)
         wide = lax.all_gather(own[rows], "feat", axis=1, tiled=True)
         halves = jnp.stack(jnp.split(wide, ways, axis=1))
         mine = lax.all_to_all(halves, "dp", split_axis=0, concat_axis=0, tiled=True)
         mine = mine.reshape(ways * step, -1)
-        part = jnp.dot(mine, weight, preferred_element_type=jnp.float32).astype(jnp.bfloat16)
+        part = dot(mine, weight).astype(jnp.bfloat16)
         parts = lax.all_to_all(
             part.reshape(ways, step, -1), "dp", split_axis=0, concat_axis=0, tiled=True
         )
@@ -50,8 +393,10 @@
         P("section", "dp", "feat"),
         P("section", "feat"),
     )
+    sizes = mesh.shape
+    fits = sizes["dp"] == 2 and sizes["feat"] == 4 and sizes["section"] == 2
     return jax.shard_map(
-        on_device,
+        paired if fits else general,
         mesh=mesh,
         in_specs=placed,
         out_specs=(P(("groups", "section"), "dp", "feat"), P(("groups", "section"), "feat")),

time: 547 us -> 340 us (0.62)
  waiting for transfers between devices: 390 us -> 0 us
  Pallas kernels: 0 us -> 305 us
  matrix products: 72.4 us -> 32.8 us
  starting transfers between devices: 22.8 us -> 0 us
  other arithmetic: 20.2 us -> 0 us
  local copies, waits for them, and re-layouts: 21.4 us -> 2.2 us
  between operations: 13.9 us -> 0.65 us
  blocking collectives: 5.82 us -> 0 us
    pallas_call x0 -> x1, Pallas kernels: none -> 305 us  [paired(): pl.pallas_call(functools.partial(exchange_kernel, CHUNKS, factor), out_sh...]
    all_gather x5 -> x0, waiting for transfers between devices: 301 us -> none  [the longest x2 219 us: on_device(): wide = lax.all_gather(own[rows], 'feat', axis=1, tiled=True)]
    all_to_all x4 -> x0, waiting for transfers between devices: 86.8 us -> none  [the longest x2 50.7 us: on_device(): mine = lax.all_to_all(halves, 'dp', split_axis=0, concat_axis=0, tiled=True)]
    dot_general x3 -> x1, matrix products: 72.4 us -> 32.8 us  [paired(): lax.dot_general(x_all, e_all, (((1,), (0,)), ((), ())), preferred_element...]
    all_to_all x4 -> x0, starting transfers between devices: 22.6 us -> none  [the longest x2 13.3 us: on_device(): mine = lax.all_to_all(halves, 'dp', split_axis=0, concat_axis=0, tiled=True)]
    reduce_sum x3 -> x0, other arithmetic: 10.3 us -> none  [the longest x2 5.6 us: on_device(): product = jnp.sum(parts.astype(jnp.float32), axis=0)]
    gather x1 -> x0, local copies, waits for them, and re-layouts: 8.63 us -> none  [on_device(): targets = gathered_final[final_order].astype(jnp.float32)]
    another operation x2 -> x0, local copies, waits for them, and re-layouts: 6.55 us -> none  [on_device(): halves = jnp.stack(jnp.split(wide, ways, axis=1))]
  transfers between devices with their start and end apart: 9 -> 0, of which waited for: 7 -> 0; matrix products, arithmetic and copies ran while one was open for 12% -> 0% of each run, Pallas kernels for 0% -> 0%
where the time goes in v2:
time: 340 us
  Pallas kernels  305 us (90%)
  matrix products  32.8 us (10%)
    pallas_call x1, Pallas kernels, paired(): pl.pallas_call(functools.partial(exchange_kernel, CHUNKS, factor), out_sh...  305 us
    dot_general x1, matrix products, paired(): lax.dot_general(x_all, e_all, (((1,), (0,)), ((), ())), preferred_element...  32.8 us

profile of v2, /device:TPU:0, one launch (start us, length us, event | category | flops | bytes accessed | tf_op | source)
XLA Modules:
  0.0 340.2 jit_solution(12308144242960483715)
XLA Ops:
  0.6 1.6 broadcast_in_dim.4.order_ref
  2.2 304.5 %exchange.1 = (bf16[2,2,768,2048]{3,2,1,0:T(8,128)(2,1)}, bf16[2,768,2048]{2,1,0:T(8,128)(2,1)}, f32[1,2048]{1,0:T(1,128)}) custom-call(bf16[768,2048]{1,0:T(8,128)(2,1)} %bitcast.11, bf16[384,2048]{1,0:T(8,128)(2,1)} %fin_hbm.1, s32[768,1]{1,0:T(8,128)} %broadcast_in_dim.4.order_ref, bf16[2,2048,2048]{2,1,0:T(8,128)(2,1)} %bitcast.10, f32[1,2048]{1,0:T(1,128)} %bias_ref.1), custom_call_target="tpu_custom_call" | custom-call | tf_op jit(solution)/shard_map/exchange/pallas_call | solution.py:312
  306.8 0.0 copy-start
  306.8 32.8 %bitcast_convert_fusion = bf16[2,2048,2048]{2,1,0:T(8,128)(2,1)} fusion(bf16[2,2,768,2048]{3,2,1,0:T(8,128)(2,1)} %get-tuple-element.5, bf16[2,768,2048]{2,1,0:T(8,128)(2,1)} %get-tuple-element.6), kind=kOutput, calls=%fused_computation | convolution fusion | flops 25778192384 | bytes 35651584 | tf_op jit(solution)/shard_map/dot_general | solution.py:347
  339.6 0.0 copy-done
  339.6 0.6 copy.13
Async XLA Ops:
  306.8 32.8 %copy-start = (f32[1,2048]{1,0:T(1,128)S(1)}, f32[1,2048]{1,0:T(1,128)}, u32[]{:S(2)}) copy-start(f32[1,2048]{1,0:T(1,128)} %get-tuple-element.11) | copy-start | bytes 24580

commit v3 on v2

--- a/solution.py
+++ b/solution.py
@@ -8,7 +8,8 @@
 from jax.experimental.pallas import tpu as pltpu
 from jax.sharding import PartitionSpec as P
 
-CHUNKS = 6
+CHUNKS = 12
+EARLY = 8
 MESH = pl.DeviceIdType.MESH
 
 
@@ -17,10 +18,10 @@
 
 
 def exchange_kernel(
-    chunks, factor, own_hbm, fin_hbm, order_ref, w_hbm, bias_ref,
-    x_out, e_out, gb_out,
-    slabs, transit, own, fin, w, p_send, p_recv, mine, err, gb,
-    load_sem, fin_sem, send_sem, recv_sem, p_sem, e_sem, gb_sem, out_sem,
+    chunks, early, factor, own_hbm, fin_hbm, order_ref, w_hbm, bias_ref,
+    x_out, e_out, gb_out, part_out,
+    slabs, transit, own, fin, w, p_send, p_recv, mine, err, gb, stage,
+    load_sem, fin_sem, send_sem, recv_sem, p_sem, e_sem, gb_sem, out_sem, part_sem,
 ):
     h = lax.axis_index("dp")
     f = lax.axis_index("feat")
@@ -216,30 +217,26 @@
 
     def keep_x(c):
         return pltpu.make_async_copy(
-            slabs.at[:, :, rows(c)], x_out.at[:, :, rows(c)], out_sem.at[c])
+            slabs.at[:, :, rows(c)], x_out.at[:, :, rows(c - early)], out_sem.at[c])
 
     tile = min(512, width)
 
     def compute(c):
         collect(c)
-        keep_x(c).start()
+        pl.when(c >= early)(keep_x(c).start)
+
+        chosen = order_ref[rows(c)] == lax.broadcasted_iota(jnp.int32, (step, tokens), 1)
+        chosen = jnp.where(chosen, 1.0, 0.0).astype(fin.dtype)
 
         @pl.loop(0, width // tile)
         def _(n):
             cols = pl.ds(pl.multiple_of(n * tile, tile), tile)
-            other = dot(slabs[0, 1, rows(c)], w[0, :, cols]) + dot(slabs[1, 1, rows(c)], w[1, :, cols])
-            p_send[rows(c), cols] = other.astype(p_send.dtype)
+            value = sum(dot(slabs[i, :, rows(c)].reshape(2 * step, width), w[i, :, cols]) for i in range(2))
+            p_send[rows(c), cols] = value[step:].astype(p_send.dtype)
+            target = dot(chosen, fin[:, cols])
+            mine[c % 2, :, cols] = own[rows(c), cols].astype(jnp.float32) + value[:step] + bias_ref[:, cols] - target
 
         send_p(c).start()
-        chosen = order_ref[rows(c)] == lax.broadcasted_iota(jnp.int32, (step, tokens), 1)
-        chosen = jnp.where(chosen, 1.0, 0.0).astype(fin.dtype)
-
-        @pl.loop(0, width // tile)
-        def _(n):
-            cols = pl.ds(pl.multiple_of(n * tile, tile), tile)
-            value = dot(slabs[0, 0, rows(c)], w[0, :, cols]) + dot(slabs[1, 0, rows(c)], w[1, :, cols])
-            target = dot(chosen, fin[:, cols])
-            mine[c % 2, :, cols] = own[rows(c), cols].astype(jnp.float32) + value + bias_ref[:, cols] - target
 
     def settle(c):
         send_p(c).wait_recv()
@@ -253,6 +250,34 @@
 
         send_e(c).start()
 
+    ready = early * step
+    band = stage.shape[1]
+    bands = width // band
+    breadth = min(1024, width)
+
+    def keep_part(i, q):
+        j = 2 * i + q
+        first = pl.multiple_of((j % bands) * band, band)
+        return pltpu.make_async_copy(
+            stage.at[q], part_out.at[j // bands, pl.ds(first, band)], part_sem.at[q])
+
+    def early_gradient(i):
+        for q in range(2):
+            j = 2 * i + q
+            pl.when(i > 0)(keep_part(i, q).wait)
+            first = pl.multiple_of((j % bands) * band, band)
+            left = slabs[j // bands, :, :ready, pl.ds(first, band)].reshape(2 * ready, band)
+
+            @pl.loop(0, width // breadth)
+            def _(n):
+                cols = pl.ds(pl.multiple_of(n * breadth, breadth), breadth)
+                right = err[:, :ready, cols].reshape(2 * ready, breadth)
+                value = lax.dot_general(
+                    left, right, (((0,), (0,)), ((), ())), preferred_element_type=jnp.float32)
+                stage[q, :, cols] = value.astype(stage.dtype)
+
+            keep_part(i, q).start()
+
     start_own(0)
     start_own(1)
 
@@ -277,6 +302,16 @@
         def _():
             compute(s - 1)
 
+        @pl.when(s == early + 2)
+        def _():
+            @pl.loop(0, early)
+            def _(c):
+                send_e(c).wait_recv()
+
+        @pl.when(jnp.logical_and(s >= early + 2, s < early + 2 + bands))
+        def _():
+            early_gradient(s - early - 2)
+
         @pl.when(s >= 2)
         def _():
             settle(s - 2)
@@ -290,11 +325,17 @@
     def _(c):
         finish(c)
         send_p(c).wait_send()
-        send_e(c).wait()
-        keep_x(c).wait()
+        send_e(c).wait_send()
+
+        @pl.when(c >= early)
+        def _():
+            send_e(c).wait_recv()
+            keep_x(c).wait()
 
     send_gb.wait()
-    keep_e = pltpu.make_async_copy(err, e_out, load_sem.at[0])
+    for q in range(2):
+        keep_part(bands - 1, q).wait()
+    keep_e = pltpu.make_async_copy(err.at[:, ready:], e_out, load_sem.at[0])
     keep_e.start()
     gb_out[...] = jnp.sum(gb[0] + gb[1], axis=0, keepdims=True)
     keep_e.wait()
@@ -305,19 +346,21 @@
     tokens, width = own.shape
     factor = 1.0 / math.sqrt(tokens * lax.axis_size("dp"))
     weight = translator[0].reshape(2, width, -1)
+    late = tokens - EARLY * (tokens // CHUNKS)
     bf16, f32 = own.dtype, jnp.float32
     hbm = pl.BlockSpec(memory_space=pl.ANY)
     vmem = pl.BlockSpec(memory_space=pltpu.VMEM)
     dma = pltpu.SemaphoreType.DMA
-    x_all, e_all, grad_b = pl.pallas_call(
-        functools.partial(exchange_kernel, CHUNKS, factor),
+    x_all, e_all, grad_b, part = pl.pallas_call(
+        functools.partial(exchange_kernel, CHUNKS, EARLY, factor),
         out_shape=(
-            jax.ShapeDtypeStruct((2, 2, tokens, width), bf16),
-            jax.ShapeDtypeStruct((2, tokens, width), bf16),
+            jax.ShapeDtypeStruct((2, 2, late, width), bf16),
+            jax.ShapeDtypeStruct((2, late, width), bf16),
             jax.ShapeDtypeStruct((1, width), f32),
+            jax.ShapeDtypeStruct((2, width, width), bf16),
         ),
         in_specs=[hbm, hbm, vmem, hbm, vmem],
-        out_specs=(hbm, hbm, vmem),
+        out_specs=(hbm, hbm, vmem, hbm),
         scratch_shapes=[
             pltpu.VMEM((2, 2, tokens, width), bf16),
             pltpu.VMEM((tokens, width), bf16),
@@ -329,6 +372,7 @@
             pltpu.VMEM((2, tokens // CHUNKS, width), f32),
             pltpu.VMEM((2, tokens, width), bf16),
             pltpu.VMEM((2, 8, width), f32),
+            pltpu.VMEM((2, width // 4, width), bf16),
             dma((4,)),
             dma((2,)),
             dma((8, CHUNKS)),
@@ -337,16 +381,18 @@
             dma((2, CHUNKS)),
             dma((2,)),
             dma((CHUNKS,)),
+            dma((2,)),
         ],
         compiler_params=pltpu.CompilerParams(
             collective_id=0, has_side_effects=True, vmem_limit_bytes=60 * 1024 * 1024),
         name="exchange",
     )(own, final_resid, final_order[:, None], weight, bias)
-    x_all = x_all.reshape(2, 2 * tokens, width)
-    e_all = e_all.reshape(2 * tokens, width)
+    x_all = x_all.reshape(2, 2 * late, width)
+    e_all = e_all.reshape(2 * late, width)
     grad_w = lax.dot_general(
         x_all, e_all, (((1,), (0,)), ((), ())), preferred_element_type=f32
-    ).astype(bf16)
+    )
+    grad_w = (grad_w + part.astype(f32)).astype(bf16)
     return grad_w.reshape(1, 2 * width, -1), grad_b
 
 

time: 340 us -> 280 us (0.82)
  Pallas kernels: 305 us -> 259 us
  matrix products: 32.8 us -> 17.6 us
    pallas_call x1, Pallas kernels: 305 us -> 259 us  [paired(): pl.pallas_call(functools.partial(exchange_kernel, CHUNKS, EARLY, factor),...]
    dot_general x1, matrix products: 32.8 us -> 17.6 us  [paired(): lax.dot_general(x_all, e_all, (((1,), (0,)), ((), ())), preferred_element...]
where the time goes in v3:
time: 280 us
  Pallas kernels  259 us (92%)
  matrix products  17.6 us (6%)
    pallas_call x1, Pallas kernels, paired(): pl.pallas_call(functools.partial(exchange_kernel, CHUNKS, EARLY, factor),...  259 us
    dot_general x1, matrix products, paired(): lax.dot_general(x_all, e_all, (((1,), (0,)), ((), ())), preferred_element...  17.6 us

profile of v3, /device:TPU:0, one launch (start us, length us, event | category | flops | bytes accessed | tf_op | source)
XLA Modules:
  0.0 279.8 jit_solution(17528006053564731851)
XLA Ops:
  0.6 1.6 broadcast_in_dim.4.order_ref
  2.2 259.4 %exchange.1 = (bf16[2,2,256,2048]{3,2,1,0:T(8,128)(2,1)}, bf16[2,256,2048]{2,1,0:T(8,128)(2,1)}, f32[1,2048]{1,0:T(1,128)}, bf16[2,2048,2048]{2,1,0:T(8,128)(2,1)}) custom-call(bf16[768,2048]{1,0:T(8,128)(2,1)} %bitcast.13, bf16[384,2048]{1,0:T(8,128)(2,1)} %fin_hbm.1, s32[768,1]{1,0:T(8,128)} %broadcast_in_dim.4.order_ref, bf16[2,2048,2048]{2,1,0:T(8,128)(2,1)} %bitcast.12, ...), custom_call_target="tpu_custom_call" | custom-call | tf_op jit(solution)/shard_map/exchange/pallas_call | solution.py:354
  261.7 0.0 copy-start
  261.7 17.6 %fusion = bf16[2,2048,2048]{2,1,0:T(8,128)(2,1)} fusion(bf16[2,2048,2048]{2,1,0:T(8,128)(2,1)} %get-tuple-element.8, bf16[2,2,256,2048]{3,2,1,0:T(8,128)(2,1)} %get-tuple-element.6, bf16[2,256,2048]{2,1,0:T(8,128)(2,1)} %get-tuple-element.7), kind=kOutput, calls=%fused_computation.1 | convolution fusion | flops 8615100416 | bytes 39845888 | tf_op jit(solution)/shard_map/dot_general | solution.py:392
  279.2 0.0 copy-done
  279.2 0.6 copy.13
Async XLA Ops:
  261.7 17.6 %copy-start = (f32[1,2048]{1,0:T(1,128)S(1)}, f32[1,2048]{1,0:T(1,128)}, u32[]{:S(2)}) copy-start(f32[1,2048]{1,0:T(1,128)} %get-tuple-element.13) | copy-start | bytes 24580
